TPU v7x, 32 devices: a whole 2x2x4 slice. The times are simulated.
32 devices in a mesh: groups: 2 (over x), width: 16 (over z, y, core).
Axes of the slice: x: 2, y: 2, z: 4, core: 2. Of those that a mesh axis runs over, the one named last changes fastest.
Arguments:
- stream_in: bfloat16 [2, 128, 8192], P(None, 'groups', 'width'), parts along dimension 1, may hold values from -16 to 16
- norm_gain: float32 [2, 8192], replicated, may hold values from 0.1 to 1.9
- w_gate: bfloat16 [2, 8192, 14336], P(None, None, 'width'), may hold values from -0.0625 to 0.0625
- w_up: bfloat16 [2, 8192, 14336], P(None, None, 'width'), may hold values from -0.0625 to 0.0625
- w_down: bfloat16 [2, 14336, 8192], P(None, 'width'), may hold values from -0.0625 to 0.0625
Outputs:
- stream_out: bfloat16 [2, 128, 8192], P(None, 'groups', 'width'), parts along dimension 1
There are 2 independent parts, one for each index of `groups`. A program takes and returns all parts, laid end to end along the dimension named above; an argument that names none is the same for every part. Nothing has to cross between parts.
All inputs are finite; a program needn't handle non-finite values.
Results may differ from a plain program's by a relative error of at most 0.012.
Values may be sent and summed in bfloat16 or wider, within the bound.
A program may use at most 192 MiB of HBM per device.

v0:
```python
import jax
import jax.numpy as jnp
from jax import lax
from jax.sharding import PartitionSpec as P

LAYERS = 2
MICRO = 2


def body(stream_in, norm_gain, w_gate, w_up, w_down):
    width_local = stream_in.shape[2]
    offset = lax.axis_index("width") * width_local
    starts = [
        lax.all_gather(stream_in[micro_index], "width", axis=1, tiled=True)
        for micro_index in range(MICRO)
    ]
    results = []
    for micro_index in range(MICRO):
        stream = starts[micro_index]
        for depth in range(LAYERS):
            stream_f = stream.astype(jnp.float32)
            meansq = jnp.mean(stream_f * stream_f, axis=1, keepdims=True)
            normed = (stream_f * lax.rsqrt(meansq + 1e-05) * norm_gain[depth]).astype(jnp.bfloat16)
            gate_out = jnp.dot(normed, w_gate[depth], preferred_element_type=jnp.float32)
            up_out = jnp.dot(normed, w_up[depth], preferred_element_type=jnp.float32)
            hidden = (jax.nn.silu(gate_out) * up_out).astype(jnp.bfloat16)
            partials = jnp.dot(hidden, w_down[depth], preferred_element_type=jnp.float32)
            branch = lax.psum(partials, "width")
            stream = (stream_f + branch).astype(jnp.bfloat16)
        results.append(stream)
    results = [lax.dynamic_slice_in_dim(stream, offset, width_local, 1) for stream in results]
    return jnp.stack(results)


def solution(mesh):
    return jax.shard_map(
        body,
        mesh=mesh,
        in_specs=(
            P(None, "groups", "width"),
            P(),
            P(None, None, "width"),
            P(None, None, "width"),
            P(None, "width", None),
        ),
        out_specs=P(None, "groups", "width"),
        check_vma=False,
    )
```

profile of v0, /device:TPU:0, one launch (start us, length us, event | category | flops | bytes accessed | tf_op | source)
XLA Modules:
  0.0 415.5 jit_solution(16510495588360910265)
XLA Ops:
  6.5 0.0 all-gather.5.cloned.1.call-start
  6.5 1.5 fusion.118
  8.1 0.0 all-gather.5.cloned.1.call-update
  8.1 0.0 all-gather.7.cloned.1.call-start
  8.1 0.7 all-gather.7.cloned.1.call-update
  8.8 0.0 all-reduce.7.cloned.1.call-start
  8.9 1.0 fusion.119
  9.9 39.0 %all-gather.5.cloned.1.call-done = bf16[1,64,8192]{2,1,0:T(8,128)(2,1)} async-done(((bf16[1,64,512]{2,1,0:T(8,128)(2,1)}), bf16[1,64,8192]{2,1,0:T(8,128)(2,1)}) %all-gather.5.cloned.1.call-update) | async-done | bytes 1048592 | tf_op jit(solution)/shard_map/all_gather | solution.py:14
  48.9 0.0 copy-start
  48.9 1.6 fusion.36
  50.5 36.8 %all-gather.7.cloned.1.call-done = bf16[1,64,8192]{2,1,0:T(8,128)(2,1)} async-done(((bf16[1,64,512]{2,1,0:T(8,128)(2,1)}), bf16[1,64,8192]{2,1,0:T(8,128)(2,1)}) %all-gather.7.cloned.1.call-update) | async-done | bytes 1048592 | tf_op jit(solution)/shard_map/all_gather | solution.py:14
  87.3 1.5 fusion.40
  88.9 0.0 copy-done
  88.9 0.0 copy-start.1
  88.9 6.7 %fusion.22 = f32[64,896]{1,0:T(8,128)S(1)} fusion(bf16[2,8192,896]{2,1,0:T(8,128)(2,1)} %param.7, bf16[1,64,8192]{2,1,0:T(8,128)(2,1)S(1)} %copy-done, f32[8192]{0:T(1024)S(1)} %bitcast.82, f32[64]{0:T(128)S(1)} %add_rsqrt_fusion.3), kind=kOutput, calls=%fused_computation.22 | convolution fusion | flops 941621248 | bytes 15991040 | tf_op jit(solution)/shard_map/dot_general | solution.py:24
  95.6 0.0 copy-done.1
  95.6 6.6 %fusion.20 = f32[64,896]{1,0:T(8,128)S(1)} fusion(bf16[2,8192,896]{2,1,0:T(8,128)(2,1)} %param.7, bf16[1,64,8192]{2,1,0:T(8,128)(2,1)S(1)} %copy-done.1, f32[64]{0:T(128)S(1)} %add_rsqrt_fusion.1, f32[8192]{0:T(1024)S(1)} %bitcast.83), kind=kOutput, calls=%fused_computation.20 | convolution fusion | flops 941621248 | bytes 15991040 | tf_op jit(solution)/shard_map/dot_general | solution.py:24
  102.2 16.4 %fusion.14 = f32[64,8192]{1,0:T(8,128)} fusion(bf16[2,896,8192]{2,1,0:T(8,128)(2,1)} %param.9, bf16[2,8192,896]{2,1,0:T(8,128)(2,1)} %param.8, bf16[1,64,8192]{2,1,0:T(8,128)(2,1)S(1)} %copy-done, f32[8192]{0:T(1024)S(1)} %bitcast.84, f32[64]{0:T(128)S(1)} %add_rsqrt_fusion.3, f32[64,896]{1,0:T(8,128)S(1)} %fusion.22), kind=kOutput, calls=%fused_computation.14 | convolution fusion | flops 1881489408 | bytes 32768256 | tf_op jit(solution)/shard_map/dot_general | solution.py:27
  118.6 16.3 %fusion.12 = f32[64,8192]{1,0:T(8,128)} fusion(bf16[2,896,8192]{2,1,0:T(8,128)(2,1)} %param.9, bf16[2,8192,896]{2,1,0:T(8,128)(2,1)} %param.8, bf16[1,64,8192]{2,1,0:T(8,128)(2,1)S(1)} %copy-done.1, f32[64]{0:T(128)S(1)} %add_rsqrt_fusion.1, f32[8192]{0:T(1024)S(1)} %bitcast.85, f32[64,896]{1,0:T(8,128)S(1)} %fusion.20), kind=kOutput, calls=%fused_computation.12 | convolution fusion | flops 1881489408 | bytes 32768256 | tf_op jit(solution)/shard_map/dot_general | solution.py:27
  134.9 0.0 all-reduce.7.cloned.1.call-update
  134.9 0.2 all-reduce.5.cloned.1.call-start
  135.2 110.9 %all-reduce.7.cloned.1.call-done = (f32[64,8192]{1,0:T(8,128)}, f32[64,8192]{1,0:T(8,128)}) async-done(((f32[64,8192]{1,0:T(8,128)}, f32[64,8192]{1,0:T(8,128)}), (f32[64,8192]{1,0:T(8,128)}, f32[64,8192]{1,0:T(8,128)})) %all-reduce.7.cloned.1.call-update) | async-done | bytes 4194320 | tf_op jit(solution)/shard_map/psum | solution.py:28
  246.0 4.2 %multiply_reduce_fusion = (f32[64]{0:T(128)S(1)}, f32[64,8192]{1,0:T(8,128)}, f32[64]{0:T(128)S(1)}, f32[64,8192]{1,0:T(8,128)S(1)}) fusion(f32[64,8192]{1,0:T(8,128)} %get-tuple-element.7, bf16[1,64,8192]{2,1,0:T(8,128)(2,1)S(1)} %copy-done.1, f32[64,8192]{1,0:T(8,128)} %get-tuple-element.8, bf16[1,64,8192]{2,1,0:T(8,128)(2,1)S(1)} %copy-done), kind=kLoop, calls=%fused_computation.51 | loop fusion | flops 6291328 | bytes 10486272 | tf_op jit(solution)/shard_map/reduce_sum | solution.py:22
  250.2 0.0 copy-start.3
  250.2 1.3 copy-done.3
  251.6 6.6 %fusion.10 = f32[64,896]{1,0:T(8,128)S(1)} fusion(bf16[2,8192,896]{2,1,0:T(8,128)(2,1)} %param.7, f32[64,8192]{1,0:T(8,128)S(1)} %get-tuple-element.18, f32[8192]{0:T(1024)S(1)} %bitcast.78, f32[64]{0:T(128)S(1)} %add_rsqrt_fusion.2), kind=kOutput, calls=%fused_computation.10 | convolution fusion | flops 941096960 | bytes 17039616 | tf_op jit(solution)/shard_map/dot_general | solution.py:24
  258.2 0.0 copy-start.2
  258.2 14.6 %fusion.2 = f32[64,8192]{1,0:T(8,128)} fusion(bf16[2,896,8192]{2,1,0:T(8,128)(2,1)} %param.9, bf16[2,8192,896]{2,1,0:T(8,128)(2,1)} %param.8, f32[64,896]{1,0:T(8,128)S(1)} %fusion.10, f32[64,8192]{1,0:T(8,128)} %copy-done.3, f32[8192]{0:T(1024)S(1)} %bitcast.79, f32[64]{0:T(128)S(1)} %add_rsqrt_fusion.2), kind=kOutput, calls=%fused_computation.2 | convolution fusion | flops 1880965120 | bytes 33816832 | tf_op jit(solution)/shard_map/dot_general | solution.py:27
  272.8 0.0 copy-done.2
  272.8 6.6 %fusion.8 = f32[64,896]{1,0:T(8,128)S(1)} fusion(bf16[2,8192,896]{2,1,0:T(8,128)(2,1)} %param.7, f32[64,8192]{1,0:T(8,128)S(1)} %copy-done.2, f32[64]{0:T(128)S(1)} %add_rsqrt_fusion, f32[8192]{0:T(1024)S(1)} %bitcast.80), kind=kOutput, calls=%fused_computation.8 | convolution fusion | flops 941096960 | bytes 17039616 | tf_op jit(solution)/shard_map/dot_general | solution.py:24
  279.5 16.4 %fusion = f32[64,8192]{1,0:T(8,128)} fusion(bf16[2,896,8192]{2,1,0:T(8,128)(2,1)} %param.9, bf16[2,8192,896]{2,1,0:T(8,128)(2,1)} %param.8, f32[64,896]{1,0:T(8,128)S(1)} %fusion.8, f32[64,8192]{1,0:T(8,128)S(1)} %copy-done.2, f32[64]{0:T(128)S(1)} %add_rsqrt_fusion, f32[8192]{0:T(1024)S(1)} %bitcast.81), kind=kOutput, calls=%fused_computation | convolution fusion | flops 1880965120 | bytes 33816832 | tf_op jit(solution)/shard_map/dot_general | solution.py:27
  295.8 0.0 all-reduce.5.cloned.1.call-update
  295.9 110.6 %all-reduce.5.cloned.1.call-done = (f32[64,8192]{1,0:T(8,128)}, f32[64,8192]{1,0:T(8,128)}) async-done(((f32[64,8192]{1,0:T(8,128)}, f32[64,8192]{1,0:T(8,128)}), (f32[64,8192]{1,0:T(8,128)}, f32[64,8192]{1,0:T(8,128)})) %all-reduce.5.cloned.1.call-update) | async-done | bytes 4194320 | tf_op jit(solution)/shard_map/psum | solution.py:28
  406.4 1.0 fusion.110
  407.4 0.9 fusion.111
  408.3 0.7 pad_maximum_fusion
  (4 shorter events, 0.0 us)
Async XLA Ops:
  6.5 42.4 %all-gather.5.cloned.1.call-start = ((), (), s32[]{:S(2)}) async-start(), calls=%async_computation | async-start | bytes 1114112 | tf_op jit(solution)/shard_map/all_gather | solution.py:14
  8.1 79.3 %all-gather.7.cloned.1.call-start = ((), (), s32[]{:S(2)}) async-start(), calls=%async_computation.1 | async-start | bytes 1114112 | tf_op jit(solution)/shard_map/all_gather | solution.py:14
  8.8 237.2 %all-reduce.7.cloned.1.call-start = ((), (), s32[]{:S(2)}) async-start(), calls=%async_computation.3 | async-start | bytes 8388608 | tf_op jit(solution)/shard_map/psum | solution.py:28
  48.9 40.0 %copy-start = (bf16[1,64,8192]{2,1,0:T(8,128)(2,1)S(1)}, bf16[1,64,8192]{2,1,0:T(8,128)(2,1)}, u32[]{:S(2)}) copy-start(bf16[1,64,8192]{2,1,0:T(8,128)(2,1)} %all-gather.5.cloned.1.call-done) | copy-start | bytes 3145732
  88.9 6.7 %copy-start.1 = (bf16[1,64,8192]{2,1,0:T(8,128)(2,1)S(1)}, bf16[1,64,8192]{2,1,0:T(8,128)(2,1)}, u32[]{:S(2)}) copy-start(bf16[1,64,8192]{2,1,0:T(8,128)(2,1)} %all-gather.7.cloned.1.call-done) | copy-start | bytes 3145732
  134.9 271.5 %all-reduce.5.cloned.1.call-start = ((), (), s32[]{:S(2)}) async-start(), calls=%async_computation.2 | async-start | bytes 8388608 | tf_op jit(solution)/shard_map/psum | solution.py:28
  250.2 1.4 copy-start.3
  258.2 14.6 %copy-start.2 = (f32[64,8192]{1,0:T(8,128)S(1)}, f32[64,8192]{1,0:T(8,128)}, u32[]{:S(2)}) copy-start(f32[64,8192]{1,0:T(8,128)} %get-tuple-element.12) | copy-start | bytes 6291460
Sparse Core Ops, SparseCore 0:
  9.5 39.3 all-gather.4
  51.0 36.2 all-gather.6
  135.1 110.9 all-reduce.6
  296.0 110.3 all-reduce.4
where the time goes:
time: 416 us
  waiting for transfers between devices  298 us (72%)
  matrix products  90.2 us (22%)
  between operations  13.2 us (3%)
  other arithmetic  9.94 us (2%)
    psum x2, waiting for transfers between devices, body(): branch = lax.psum(partials, 'width')  221 us
    all_gather x2, waiting for transfers between devices, body(): lax.all_gather(stream_in[micro_index], 'width', axis=1, tiled=True)  75.8 us
    dot_general x4, matrix products, body(): jnp.dot(hidden, w_down[depth], preferred_element_type=jnp.float32)  63.7 us
    dot_general x4, matrix products, body(): jnp.dot(normed, w_gate[depth], preferred_element_type=jnp.float32)  26.5 us
  transfers between devices with their start and end apart: 4, of which 4 were waited for; matrix products, arithmetic and copies ran while one was open for 1% of the time, Pallas kernels for 0%

commit v1 on v0

--- a/solution.py
+++ b/solution.py
@@ -7,12 +7,17 @@
 MICRO = 2
 
 
+def gather_by_exchange(x, axis, dim):
+    length = lax.axis_size(axis)
+    repeats = [length if d == dim else 1 for d in range(x.ndim)]
+    return lax.all_to_all(jnp.tile(x, repeats), axis, split_axis=dim, concat_axis=dim, tiled=True)
+
+
 def body(stream_in, norm_gain, w_gate, w_up, w_down):
     width_local = stream_in.shape[2]
     offset = lax.axis_index("width") * width_local
     starts = [
-        lax.all_gather(stream_in[micro_index], "width", axis=1, tiled=True)
-        for micro_index in range(MICRO)
+        gather_by_exchange(stream_in[micro_index], "width", 1) for micro_index in range(MICRO)
     ]
     results = []
     for micro_index in range(MICRO):

time: 416 us -> 403 us (0.969)
  waiting for transfers between devices: 298 us -> 244 us
  blocking collectives: 0 us -> 31.9 us
  starting transfers between devices: 0.3 us -> 5.11 us
    all_gather x2 -> x0, waiting for transfers between devices: 75.8 us -> none  [body(): lax.all_gather(stream_in[micro_index], 'width', axis=1, tiled=True)]
    all_to_all x0 -> x1, blocking collectives: none -> 31.9 us  [gather_by_exchange(): lax.all_to_all(jnp.tile(x, repeats), axis, split_axis=dim, concat_axis=di...]
    all_to_all x0 -> x1, waiting for transfers between devices: none -> 22.4 us  [gather_by_exchange(): lax.all_to_all(jnp.tile(x, repeats), axis, split_axis=dim, concat_axis=di...]
    all_to_all x0 -> x1, starting transfers between devices: none -> 5.02 us  [gather_by_exchange(): lax.all_to_all(jnp.tile(x, repeats), axis, split_axis=dim, concat_axis=di...]
  transfers between devices with their start and end apart: 4 -> 3, of which waited for: 4 -> 3; matrix products, arithmetic and copies ran while one was open for 1% -> 1% of each run, Pallas kernels for 0% -> 0%
where the time goes in v1:
time: 403 us; the launch traced here: 402 us
  waiting for transfers between devices  244 us (61%)
  matrix products  93 us (23%)
  blocking collectives  31.9 us (8%)
  between operations  13.6 us (3%)
  other arithmetic  9.25 us (2%)
  local copies, waits for them, and re-layouts  5.48 us (1%)
  starting transfers between devices  5.11 us (1%)
    psum x2, waiting for transfers between devices, body(): branch = lax.psum(partials, 'width')  221 us
    dot_general x4, matrix products, body(): jnp.dot(hidden, w_down[depth], preferred_element_type=jnp.float32)  63.6 us
    all_to_all x1, blocking collectives, gather_by_exchange(): lax.all_to_all(jnp.tile(x, repeats), axis, split_axis=dim, concat_axis=di...  31.9 us
    dot_general x4, matrix products, body(): jnp.dot(normed, w_gate[depth], preferred_element_type=jnp.float32)  29.4 us
    all_to_all x1, waiting for transfers between devices, gather_by_exchange(): lax.all_to_all(jnp.tile(x, repeats), axis, split_axis=dim, concat_axis=di...  22.4 us
  transfers between devices with their start and end apart: 3, of which 3 were waited for; matrix products, arithmetic and copies ran while one was open for 1% of the time, Pallas kernels for 0%

profile of v1, /device:TPU:0, one launch (start us, length us, event | category | flops | bytes accessed | tf_op | source)
XLA Modules:
  0.0 402.3 jit_solution(13399095424059408358)
XLA Ops:
  6.5 0.9 slice_bitcast_fusion.1
  7.4 0.1 tile.19
  7.5 31.9 %all_to_all.12 = bf16[64,16,512]{2,0,1:T(8,128)(2,1)S(1)} all-to-all(bf16[64,16,512]{2,0,1:T(8,128)(2,1)S(1)} %tile.19), channel_id=1, replica_groups=mesh['groups'=2,'width'=16] {'width'}, dimensions={1} | all-to-all | bytes 2097152 | tf_op jit(solution)/shard_map/all_to_all | solution.py:13
  39.4 0.0 copy-start.3
  39.4 1.1 tile.17
  40.5 5.0 %all-to-all-start = ((bf16[64,16,512]{2,0,1:T(8,128)(2,1)}), bf16[64,16,512]{2,0,1:T(8,128)(2,1)S(1)}, u32[]{:S(2)}, u32[]{:S(2)}) async-start(bf16[64,16,512]{2,0,1:T(8,128)(2,1)} %tile.17), calls=%async_computation | async-start | bytes 2097152 | tf_op jit(solution)/shard_map/all_to_all | solution.py:13
  45.5 0.0 all-reduce.7.cloned.1.call-start
  45.6 0.0 copy-done.3
  45.6 0.1 fusion.112
  45.7 0.3 fusion.39
  46.0 22.4 %all-to-all-done = bf16[64,16,512]{2,0,1:T(8,128)(2,1)S(1)} async-done(((bf16[64,16,512]{2,0,1:T(8,128)(2,1)}), bf16[64,16,512]{2,0,1:T(8,128)(2,1)S(1)}, u32[]{:S(2)}, u32[]{:S(2)}) %all-to-all-start) | async-done | bytes 1048608 | tf_op jit(solution)/shard_map/all_to_all | solution.py:13
  68.4 0.3 fusion.36
  68.8 0.7 fusion.69
  69.4 0.1 copy.13
  69.5 0.1 copy.15
  69.6 0.0 copy-start.2
  69.6 8.6 %fusion.22 = f32[64,896]{1,0:T(8,128)} fusion(bf16[64,8192]{1,0:T(8,128)(2,1)S(1)} %bitcast.81, bf16[2,8192,896]{2,1,0:T(8,128)(2,1)} %param.7), kind=kOutput, calls=%fused_computation.22 | convolution fusion | flops 939524096 | bytes 15958016 | tf_op jit(solution)/shard_map/dot_general | solution.py:29
  78.3 0.0 copy-done.2
  78.3 7.6 %fusion.20 = f32[64,896]{1,0:T(8,128)S(1)} fusion(bf16[64,8192]{1,0:T(8,128)(2,1)S(1)} %bitcast.83, bf16[2,8192,896]{2,1,0:T(8,128)(2,1)} %param.7), kind=kOutput, calls=%fused_computation.20 | convolution fusion | flops 939524096 | bytes 15958016 | tf_op jit(solution)/shard_map/dot_general | solution.py:29
  85.9 16.1 %fusion.14 = f32[64,8192]{1,0:T(8,128)} fusion(bf16[2,896,8192]{2,1,0:T(8,128)(2,1)} %param.9, bf16[64,8192]{1,0:T(8,128)(2,1)S(1)} %bitcast.82, bf16[2,8192,896]{2,1,0:T(8,128)(2,1)} %param.8, f32[64,896]{1,0:T(8,128)} %fusion.22), kind=kOutput, calls=%fused_computation.14 | convolution fusion | flops 1879392256 | bytes 32735232 | tf_op jit(solution)/shard_map/dot_general | solution.py:32
  102.0 16.5 %fusion.12 = f32[64,8192]{1,0:T(8,128)} fusion(bf16[2,896,8192]{2,1,0:T(8,128)(2,1)} %param.9, bf16[64,8192]{1,0:T(8,128)(2,1)} %bitcast.84, bf16[2,8192,896]{2,1,0:T(8,128)(2,1)} %param.8, f32[64,896]{1,0:T(8,128)S(1)} %fusion.20), kind=kOutput, calls=%fused_computation.12 | convolution fusion | flops 1879392256 | bytes 32735232 | tf_op jit(solution)/shard_map/dot_general | solution.py:32
  118.5 0.0 all-reduce.7.cloned.1.call-update
  118.5 0.0 all-reduce.5.cloned.1.call-start
  118.5 0.3 convert_bitcast_fusion.1
  118.8 0.2 copy.12
  119.0 0.3 convert_bitcast_fusion
  119.3 1.6 copy.14
  120.9 111.1 %all-reduce.7.cloned.1.call-done = (f32[64,8192]{1,0:T(8,128)}, f32[64,8192]{1,0:T(8,128)}) async-done(((f32[64,8192]{1,0:T(8,128)}, f32[64,8192]{1,0:T(8,128)}), (f32[64,8192]{1,0:T(8,128)}, f32[64,8192]{1,0:T(8,128)})) %all-reduce.7.cloned.1.call-update) | async-done | bytes 4194320 | tf_op jit(solution)/shard_map/psum | solution.py:33
  232.0 4.8 %multiply_reduce_fusion = (f32[64]{0:T(128)S(1)}, f32[64,8192]{1,0:T(8,128)}, f32[64]{0:T(128)S(1)}, f32[64,8192]{1,0:T(8,128)S(1)}) fusion(f32[64,8192]{1,0:T(8,128)} %bitcast.80, f32[64,8192]{1,0:T(8,128)} %get-tuple-element.7, f32[64,8192]{1,0:T(8,128)S(1)} %bitcast.79, f32[64,8192]{1,0:T(8,128)} %get-tuple-element.8), kind=kLoop, calls=%fused_computation.49 | loop fusion | flops 5242752 | bytes 12583424 | tf_op jit(solution)/shard_map/reduce_sum | solution.py:27
  236.8 0.0 copy-start.1
  236.8 1.3 copy-done.1
  238.1 6.6 %fusion.10 = f32[64,896]{1,0:T(8,128)S(1)} fusion(bf16[2,8192,896]{2,1,0:T(8,128)(2,1)} %param.7, f32[64,8192]{1,0:T(8,128)S(1)} %get-tuple-element.20, f32[8192]{0:T(1024)S(1)} %bitcast.85, f32[64]{0:T(128)S(1)} %add_rsqrt_fusion.2), kind=kOutput, calls=%fused_computation.10 | convolution fusion | flops 941096960 | bytes 17039616 | tf_op jit(solution)/shard_map/dot_general | solution.py:29
  244.8 0.0 copy-start
  244.8 14.6 %fusion.2 = f32[64,8192]{1,0:T(8,128)} fusion(bf16[2,896,8192]{2,1,0:T(8,128)(2,1)} %param.9, bf16[2,8192,896]{2,1,0:T(8,128)(2,1)} %param.8, f32[64,896]{1,0:T(8,128)S(1)} %fusion.10, f32[64,8192]{1,0:T(8,128)} %copy-done.1, f32[8192]{0:T(1024)S(1)} %bitcast.86, f32[64]{0:T(128)S(1)} %add_rsqrt_fusion.2), kind=kOutput, calls=%fused_computation.2 | convolution fusion | flops 1880965120 | bytes 33816832 | tf_op jit(solution)/shard_map/dot_general | solution.py:32
  259.4 0.0 copy-done
  259.4 6.6 %fusion.8 = f32[64,896]{1,0:T(8,128)S(1)} fusion(bf16[2,8192,896]{2,1,0:T(8,128)(2,1)} %param.7, f32[64,8192]{1,0:T(8,128)S(1)} %copy-done, f32[64]{0:T(128)S(1)} %add_rsqrt_fusion, f32[8192]{0:T(1024)S(1)} %bitcast.87), kind=kOutput, calls=%fused_computation.8 | convolution fusion | flops 941096960 | bytes 17039616 | tf_op jit(solution)/shard_map/dot_general | solution.py:29
  266.0 16.4 %fusion = f32[64,8192]{1,0:T(8,128)} fusion(bf16[2,896,8192]{2,1,0:T(8,128)(2,1)} %param.9, bf16[2,8192,896]{2,1,0:T(8,128)(2,1)} %param.8, f32[64,896]{1,0:T(8,128)S(1)} %fusion.8, f32[64,8192]{1,0:T(8,128)S(1)} %copy-done, f32[64]{0:T(128)S(1)} %add_rsqrt_fusion, f32[8192]{0:T(1024)S(1)} %bitcast.88), kind=kOutput, calls=%fused_computation | convolution fusion | flops 1880965120 | bytes 33816832 | tf_op jit(solution)/shard_map/dot_general | solution.py:32
  282.4 0.0 all-reduce.5.cloned.1.call-update
  282.4 110.4 %all-reduce.5.cloned.1.call-done = (f32[64,8192]{1,0:T(8,128)}, f32[64,8192]{1,0:T(8,128)}) async-done(((f32[64,8192]{1,0:T(8,128)}, f32[64,8192]{1,0:T(8,128)}), (f32[64,8192]{1,0:T(8,128)}, f32[64,8192]{1,0:T(8,128)})) %all-reduce.5.cloned.1.call-update) | async-done | bytes 4194320 | tf_op jit(solution)/shard_map/psum | solution.py:33
  392.8 1.0 fusion.104
  393.8 0.9 fusion.105
  394.7 0.7 pad_maximum_fusion
  (5 shorter events, 0.0 us)
Async XLA Ops:
  39.4 6.2 %copy-start.3 = (f32[2,8192]{1,0:T(2,128)S(1)}, f32[2,8192]{1,0:T(2,128)}, u32[]{:S(2)}) copy-start(f32[2,8192]{1,0:T(2,128)} %param.6) | copy-start | bytes 196612
  40.5 27.9 %all-to-all-start = ((bf16[64,16,512]{2,0,1:T(8,128)(2,1)}), bf16[64,16,512]{2,0,1:T(8,128)(2,1)S(1)}, u32[]{:S(2)}, u32[]{:S(2)}) async-start(bf16[64,16,512]{2,0,1:T(8,128)(2,1)} %tile.17), calls=%async_computation | async-start | bytes 2097152 | tf_op jit(solution)/shard_map/all_to_all | solution.py:13
  45.5 186.4 %all-reduce.7.cloned.1.call-start = ((), (), s32[]{:S(2)}) async-start(), calls=%async_computation.3 | async-start | bytes 8388608 | tf_op jit(solution)/shard_map/psum | solution.py:33
  69.6 8.7 %copy-start.2 = (bf16[16,8,8,512]{3,2,0,1:T(8,128)(2,1)}, bf16[16,8,8,512]{3,2,0,1:T(8,128)(2,1)S(1)}, u32[]{:S(2)}) copy-start(bf16[16,8,8,512]{3,2,0,1:T(8,128)(2,1)S(1)} %copy.15) | copy-start | bytes 3145732
  118.5 274.3 %all-reduce.5.cloned.1.call-start = ((), (), s32[]{:S(2)}) async-start(), calls=%async_computation.2 | async-start | bytes 8388608 | tf_op jit(solution)/shard_map/psum | solution.py:33
  236.8 1.4 copy-start.1
  244.8 14.6 %copy-start = (f32[64,8192]{1,0:T(8,128)S(1)}, f32[64,8192]{1,0:T(8,128)}, u32[]{:S(2)}) copy-start(f32[64,8192]{1,0:T(8,128)} %get-tuple-element.12) | copy-start | bytes 6291460
Sparse Core Ops, SparseCore 0:
  118.6 113.3 all-reduce.6
  282.5 110.2 all-reduce.4
